TPU v7x, 32 devices: a whole 2x2x4 slice. The times are simulated.
32 devices in a mesh: groups: 2 (over x), blocks: 16 (over z, y, core).
Axes of the slice: x: 2, y: 2, z: 4, core: 2. Of those that a mesh axis runs over, the one named last changes fastest.
Arguments:
- activations: float32 [2048, 2048], P('blocks', 'groups'), parts along dimension 1, may hold values from -180 to 180
- cotangent: float32 [2048, 2048], P('blocks', 'groups'), parts along dimension 1, may hold values from -6 to 6
- gain: float32 [2048], P('blocks'), may hold values from 0.5 to 1.5
- left_one: float32 [16, 128, 128], P('blocks'), may hold values from -0.5 to 0.5
- right_one: float32 [128, 16, 16], P('blocks'), may hold values from -1.5 to 1.5
- left_two: float32 [16, 128, 128], P('blocks'), may hold values from -0.5 to 0.5
- right_two: float32 [128, 16, 16], P('blocks'), may hold values from -1.5 to 1.5
Outputs:
- output: float32 [2048, 2048], P('blocks', 'groups'), parts along dimension 1
- input_gradient: float32 [2048, 2048], P('blocks', 'groups'), parts along dimension 1
- gain_gradient: float32 [4096], P(('groups', 'blocks')), parts along dimension 0
- grad_left_one: float32 [32, 128, 128], P(('groups', 'blocks')), parts along dimension 0
- grad_right_one: float32 [256, 16, 16], P(('groups', 'blocks')), parts along dimension 0
- grad_left_two: float32 [32, 128, 128], P(('groups', 'blocks')), parts along dimension 0
- grad_right_two: float32 [256, 16, 16], P(('groups', 'blocks')), parts along dimension 0
There are 2 independent parts, one for each index of `groups`. A program takes and returns all parts, laid end to end along the dimension named above; an argument that names none is the same for every part. Nothing has to cross between parts.
All inputs are finite; a program needn't handle non-finite values.
Results may differ from a plain program's by a relative error of at most 0.0001.
Values sent between devices are 32-bit elements; how exact they have to be, the bound alone decides.
No kernel may reach another device: no remote copies, remote signals or barrier semaphores. Data moves between devices by JAX's collectives and lax.ppermute only.
A program may use at most 64 MiB of HBM per device.

v0:
```python
import math
import jax
import jax.numpy as jnp
from jax import lax
from jax.sharding import PartitionSpec as P

COEFF = math.sqrt(2.0 / math.pi)
EPSILON = 1e-05
HIGH = lax.Precision.HIGHEST


def gelu_value(values):
    return 0.5 * values * (1.0 + jnp.tanh(COEFF * (values + 0.044715 * values * values * values)))


def gelu_slope(values):
    tangent = jnp.tanh(COEFF * (values + 0.044715 * values * values * values))
    return 0.5 * (1.0 + tangent) + 0.5 * values * (1.0 - tangent * tangent) * COEFF * (
        1.0 + 3.0 * 0.044715 * values * values
    )


def first_factor(stacked, left):
    return jnp.einsum("bij,bit->bjt", left, stacked, precision=HIGH)


def monarch_forward(stacked, left, right):
    first = first_factor(stacked, left)
    regrouped = lax.all_to_all(first, "blocks", split_axis=1, concat_axis=0, tiled=True)
    second = jnp.einsum("jbk,bjt->jkt", right, regrouped, precision=HIGH)
    return (second, regrouped)


def monarch_backward(grad_out, stacked, left, right, regrouped, factor_matrix):
    grad_right = jnp.einsum("bjt,jkt->jbk", regrouped, grad_out, precision=HIGH) * factor_matrix
    grad_mid = jnp.einsum("jbk,jkt->bjt", right, grad_out, precision=HIGH)
    piece = lax.all_to_all(grad_mid, "blocks", split_axis=0, concat_axis=1, tiled=True)
    grad_stacked = jnp.einsum("bij,bjt->bit", left, piece, precision=HIGH)
    grad_left = jnp.einsum("bit,bjt->bij", stacked, piece, precision=HIGH) * factor_matrix
    return (grad_stacked, grad_left, grad_right)


def local(activations, cotangent, gain, left_one, right_one, left_two, right_two):
    features, tokens = activations.shape
    blocks_here = left_one.shape[0]
    block_order = left_one.shape[1]
    outer_here = right_one.shape[0]
    block_count = right_one.shape[1]
    feature_width = features * lax.axis_size("blocks")
    factor_matrix = tokens ** (-0.5)
    squares = lax.psum(jnp.sum(activations * activations, axis=0), "blocks")
    inverse_root = lax.rsqrt(squares / feature_width + EPSILON)[None, :]
    centered_input = activations * inverse_root
    normed_rows = centered_input * gain[:, None]
    normed_stacked = normed_rows.reshape(blocks_here, block_order, tokens)
    second_one, regrouped_one = monarch_forward(normed_stacked, left_one, right_one)
    pre = second_one.reshape(features, tokens)
    acted = gelu_value(pre)
    acted_stacked = acted.reshape(blocks_here, block_order, tokens)
    second_two, regrouped_two = monarch_forward(acted_stacked, left_two, right_two)
    output = activations + second_two.reshape(features, tokens)
    grad_acted, grad_left_two, grad_right_two = monarch_backward(
        cotangent.reshape(outer_here, block_count, tokens),
        acted_stacked,
        left_two,
        right_two,
        regrouped_two,
        factor_matrix,
    )
    grad_pre = grad_acted.reshape(features, tokens) * gelu_slope(pre)
    normalized_gradient, grad_left_one, grad_right_one = monarch_backward(
        grad_pre.reshape(outer_here, block_count, tokens),
        normed_stacked,
        left_one,
        right_one,
        regrouped_one,
        factor_matrix,
    )
    normalized_gradient = normalized_gradient.reshape(features, tokens)
    gradient_scaled = gain[:, None] * normalized_gradient
    inner_width = lax.psum(jnp.sum(gradient_scaled * centered_input, axis=0), "blocks")
    input_gradient = cotangent + inverse_root * (
        gradient_scaled - centered_input * (inner_width / feature_width)[None, :]
    )
    gain_gradient = jnp.sum(normalized_gradient * centered_input, axis=1) * factor_matrix
    return (
        output,
        input_gradient,
        gain_gradient,
        grad_left_one,
        grad_right_one,
        grad_left_two,
        grad_right_two,
    )


def solution(mesh):
    return jax.shard_map(
        local,
        mesh=mesh,
        in_specs=(
            P("blocks", "groups"),
            P("blocks", "groups"),
            P("blocks"),
            P("blocks", None, None),
            P("blocks", None, None),
            P("blocks", None, None),
            P("blocks", None, None),
        ),
        out_specs=(
            P("blocks", "groups"),
            P("blocks", "groups"),
            P(("groups", "blocks")),
            P(("groups", "blocks"), None, None),
            P(("groups", "blocks"), None, None),
            P(("groups", "blocks"), None, None),
            P(("groups", "blocks"), None, None),
        ),
        check_vma=False,
    )
```

profile of v0, /device:TPU:0, one launch (start us, length us, event | category | flops | bytes accessed | tf_op | source)
XLA Modules:
  0.0 149.8 jit_solution(11019445430799419862)
XLA Ops:
  0.7 1.2 multiply_reduce_fusion.2
  2.1 35.0 %psum.14 = f32[1024]{0:T(1024)S(1)} all-reduce(f32[1024]{0:T(1024)S(1)} %multiply_reduce_fusion.2), channel_id=1, replica_groups=mesh['groups'=2,'blocks'=16] {'blocks'}, use_global_device_ids=true, to_apply=%region_1.0 | all-reduce | flops 1024 | bytes 8192 | tf_op jit(solution)/shard_map/psum | solution.py:51
  37.1 0.6 copy-done.10
  37.7 0.6 convolution_bitcast_fusion.5
  38.3 1.0 copy.37
  39.4 3.7 %all-to-all-start = ((f32[1,128,1024]{2,0,1:T(1,128)}), f32[1,128,1024]{2,0,1:T(1,128)S(1)}, u32[]{:S(2)}, u32[]{:S(2)}) async-start(f32[1,128,1024]{2,0,1:T(1,128)} %copy.37), calls=%async_computation | async-start | bytes 1048576 | tf_op jit(solution)/shard_map/all_to_all | solution.py:29
  43.1 0.6 convolution_bitcast_fusion.2
  43.7 1.1 copy.43
  44.8 12.5 %all-to-all-done = f32[1,128,1024]{2,0,1:T(1,128)S(1)} async-done(((f32[1,128,1024]{2,0,1:T(1,128)}), f32[1,128,1024]{2,0,1:T(1,128)S(1)}, u32[]{:S(2)}, u32[]{:S(2)}) %all-to-all-start) | async-done | bytes 524320 | tf_op jit(solution)/shard_map/all_to_all | solution.py:29
  57.3 4.1 %all-to-all-start.2 = ((f32[16,8,1024]{2,1,0:T(8,128)}), f32[16,8,1024]{2,1,0:T(8,128)S(1)}, u32[]{:S(2)}, u32[]{:S(2)}) async-start(f32[16,8,1024]{2,1,0:T(8,128)} %copy.43), calls=%async_computation.2 | async-start | bytes 1048576 | tf_op jit(solution)/shard_map/all_to_all | solution.py:37
  61.6 1.8 %add_multiply_fusion = (f32[8,16,1024]{2,1,0:T(8,128)S(1)}, f32[8,16,1024]{2,1,0:T(8,128)}) fusion(f32[8,16,16]{2,1,0:T(8,128)S(1)} %copy-done, f32[16,8,1024]{2,1,0:T(8,128)S(1)} %bitcast.73), kind=kOutput, calls=%fused_computation.37 | convolution fusion | flops 26214400 | bytes 1581056 | tf_op jit(solution)/shard_map/jbk,bjt->jkt/dot_general | solution.py:30
  63.4 1.0 convolution_bitcast_fusion.3
  64.4 1.0 copy.40
  65.4 10.3 %all-to-all-done.2 = f32[16,8,1024]{2,1,0:T(8,128)S(1)} async-done(((f32[16,8,1024]{2,1,0:T(8,128)}), f32[16,8,1024]{2,1,0:T(8,128)S(1)}, u32[]{:S(2)}, u32[]{:S(2)}) %all-to-all-start.2) | async-done | bytes 524320 | tf_op jit(solution)/shard_map/all_to_all | solution.py:37
  75.7 4.2 %all-to-all-start.1 = ((f32[1,128,1024]{2,0,1:T(1,128)}), f32[1,128,1024]{2,0,1:T(1,128)}, u32[]{:S(2)}, u32[]{:S(2)}) async-start(f32[1,128,1024]{2,0,1:T(1,128)} %copy.40), calls=%async_computation.1 | async-start | bytes 1048576 | tf_op jit(solution)/shard_map/all_to_all | solution.py:29
  80.2 0.6 fusion.11
  81.2 0.9 convolution_bitcast_fusion.1
  82.1 1.1 copy.44
  83.2 1.2 fusion
  84.4 9.8 %all-to-all-done.1 = f32[1,128,1024]{2,0,1:T(1,128)} async-done(((f32[1,128,1024]{2,0,1:T(1,128)}), f32[1,128,1024]{2,0,1:T(1,128)}, u32[]{:S(2)}, u32[]{:S(2)}) %all-to-all-start.1) | async-done | bytes 524320 | tf_op jit(solution)/shard_map/all_to_all | solution.py:29
  94.2 4.2 %all-to-all-start.3 = ((f32[16,8,1024]{2,1,0:T(8,128)}), f32[16,8,1024]{2,1,0:T(8,128)S(1)}, u32[]{:S(2)}, u32[]{:S(2)}) async-start(f32[16,8,1024]{2,1,0:T(8,128)} %copy.44), calls=%async_computation.3 | async-start | bytes 1048576 | tf_op jit(solution)/shard_map/all_to_all | solution.py:37
  98.4 3.1 %convolution_multiply_fusion.2 = f32[8,16,16]{2,1,0:T(8,128)} fusion(f32[16,8,1024]{2,1,0:T(8,128)S(1)} %bitcast.74, f32[8,16,1024]{2,1,0:T(8,128)} %bitcast.76, f32[8,16,1024]{2,1,0:T(8,128)} %get-tuple-element.31), kind=kOutput, calls=%fused_computation.9 | convolution fusion | flops 27527168 | bytes 1581056 | tf_op jit(solution)/shard_map/bjt,jkt->jbk/dot_general | solution.py:35
  101.6 1.1 copy.65
  102.7 1.8 %convolution_multiply_fusion = f32[8,16,16]{2,1,0:T(8,128)} fusion(f32[8,16,1024]{2,1,0:T(8,128)S(1)} %bitcast.70, f32[16,8,1024]{2,1,0:T(8,128)S(1)} %bitcast.71), kind=kOutput, calls=%fused_computation.6 | convolution fusion | flops 25167872 | bytes 1056768 | tf_op jit(solution)/shard_map/bjt,jkt->jbk/dot_general | solution.py:35
  104.5 0.9 fusion.14
  105.4 0.9 bitcast_add_fusion
  106.2 6.4 %all-to-all-done.3 = f32[16,8,1024]{2,1,0:T(8,128)S(1)} async-done(((f32[16,8,1024]{2,1,0:T(8,128)}), f32[16,8,1024]{2,1,0:T(8,128)S(1)}, u32[]{:S(2)}, u32[]{:S(2)}) %all-to-all-start.3) | async-done | bytes 524320 | tf_op jit(solution)/shard_map/all_to_all | solution.py:37
  112.7 1.2 multiply_reduce_fusion
  113.9 0.5 broadcast_multiply_fusion.1
  114.4 32.2 %psum.15 = f32[1024]{0:T(1024)S(1)} all-reduce(f32[1024]{0:T(1024)S(1)} %get-tuple-element.29), channel_id=1, replica_groups=mesh['groups'=2,'blocks'=16] {'blocks'}, use_global_device_ids=true, to_apply=%region_3.0 | all-reduce | flops 1024 | bytes 8192 | tf_op jit(solution)/shard_map/psum | solution.py:81
  147.0 1.0 copy.48
  148.0 1.8 %fusion.1 = f32[1,128,128]{2,1,0:T(8,128)} fusion(f32[16,8,1024]{2,1,0:T(8,128)S(1)} %all-to-all-done.3, f32[128,1024]{0,1:T(8,128)S(1)} %copy.36, f32[128]{0:T(128)S(1)} %copy-done.10, f32[1024]{0:T(1024)S(1)} %add_rsqrt_fusion), kind=kOutput, calls=%fused_computation.11 | convolution fusion | flops 201605120 | bytes 1118720 | tf_op jit(solution)/shard_map/bit,bjt->bij/dot_general | solution.py:39
  (27 shorter events, 1.4 us)
Async XLA Ops:
  0.6 60.9 %copy-start = (f32[8,16,16]{2,1,0:T(8,128)S(1)}, f32[8,16,16]{2,1,0:T(8,128)}, u32[]{:S(2)}) copy-start(f32[8,16,16]{2,1,0:T(8,128)} %param.11) | copy-start | bytes 24580
  0.6 1.2 copy-start.1
  1.9 35.2 %copy-start.9 = (f32[1,128,128]{2,1,0:T(8,128)S(1)}, f32[1,128,128]{2,1,0:T(8,128)}, u32[]{:S(2)}) copy-start(f32[1,128,128]{2,1,0:T(8,128)} %param.10) | copy-start | bytes 196612
  37.0 0.7 copy-start.10
  39.4 3.7 %copy-start.2 = (f32[128,1024]{1,0:T(8,128)S(1)}, f32[128,1024]{1,0:T(8,128)}, u32[]{:S(2)}) copy-start(f32[128,1024]{1,0:T(8,128)} %param.8) | copy-start | bytes 1572868
  39.4 3.7 %copy-start.8 = (f32[8,16,16]{2,1,0:T(8,128)S(1)}, f32[8,16,16]{2,1,0:T(8,128)}, u32[]{:S(2)}) copy-start(f32[8,16,16]{2,1,0:T(8,128)} %param.13) | copy-start | bytes 24580
  39.4 17.9 %all-to-all-start = ((f32[1,128,1024]{2,0,1:T(1,128)}), f32[1,128,1024]{2,0,1:T(1,128)S(1)}, u32[]{:S(2)}, u32[]{:S(2)}) async-start(f32[1,128,1024]{2,0,1:T(1,128)} %copy.37), calls=%async_computation | async-start | bytes 1048576 | tf_op jit(solution)/shard_map/all_to_all | solution.py:29
  57.3 18.4 %all-to-all-start.2 = ((f32[16,8,1024]{2,1,0:T(8,128)}), f32[16,8,1024]{2,1,0:T(8,128)S(1)}, u32[]{:S(2)}, u32[]{:S(2)}) async-start(f32[16,8,1024]{2,1,0:T(8,128)} %copy.43), calls=%async_computation.2 | async-start | bytes 1048576 | tf_op jit(solution)/shard_map/all_to_all | solution.py:37
  61.5 1.8 %copy-start.3 = (f32[1,128,1024]{2,1,0:T(8,128)}, f32[1,128,1024]{2,1,0:T(8,128)S(1)}, u32[]{:S(2)}) copy-start(f32[1,128,1024]{2,1,0:T(8,128)S(1)} %copy.66) | copy-start | bytes 1572868
  61.5 1.8 %copy-start.7 = (f32[1,128,128]{2,1,0:T(8,128)S(1)}, f32[1,128,128]{2,1,0:T(8,128)}, u32[]{:S(2)}) copy-start(f32[1,128,128]{2,1,0:T(8,128)} %param.12) | copy-start | bytes 196612
  75.7 18.5 %all-to-all-start.1 = ((f32[1,128,1024]{2,0,1:T(1,128)}), f32[1,128,1024]{2,0,1:T(1,128)}, u32[]{:S(2)}, u32[]{:S(2)}) async-start(f32[1,128,1024]{2,0,1:T(1,128)} %copy.40), calls=%async_computation.1 | async-start | bytes 1048576 | tf_op jit(solution)/shard_map/all_to_all | solution.py:29
  80.1 1.0 copy-start.5
  80.8 1.3 copy-start.6
  84.4 14.0 %copy-start.4 = (f32[1,128,1024]{2,1,0:T(8,128)S(1)}, f32[1,128,1024]{2,1,0:T(8,128)}, u32[]{:S(2)}) copy-start(f32[1,128,1024]{2,1,0:T(8,128)} %copy-done.3) | copy-start | bytes 1572868
  94.2 18.4 %all-to-all-start.3 = ((f32[16,8,1024]{2,1,0:T(8,128)}), f32[16,8,1024]{2,1,0:T(8,128)S(1)}, u32[]{:S(2)}, u32[]{:S(2)}) async-start(f32[16,8,1024]{2,1,0:T(8,128)} %copy.44), calls=%async_computation.3 | async-start | bytes 1048576 | tf_op jit(solution)/shard_map/all_to_all | solution.py:37
where the time goes:
time: 151 us; the launch traced here: 150 us
  blocking collectives  67.2 us (45%)
  waiting for transfers between devices  39.1 us (26%)
  starting transfers between devices  16.2 us (11%)
  matrix products  15.5 us (10%)
  local copies, waits for them, and re-layouts  8.06 us (5%)
  other arithmetic  2.89 us (2%)
    psum x1, blocking collectives, local(): squares = lax.psum(jnp.sum(activations * activations, axis=0), 'blocks')  35 us
    psum x1, blocking collectives, local(): lax.psum(jnp.sum(gradient_scaled * centered_input, axis=0), 'blocks')  32.2 us
    all_to_all x2, waiting for transfers between devices, monarch_forward(): lax.all_to_all(first, 'blocks', split_axis=1, concat_axis=0, tiled=True)  22.3 us
    all_to_all x2, waiting for transfers between devices, monarch_backward(): lax.all_to_all(grad_mid, 'blocks', split_axis=0, concat_axis=1, tiled=True)  16.7 us
    all_to_all x2, starting transfers between devices, monarch_backward(): lax.all_to_all(grad_mid, 'blocks', split_axis=0, concat_axis=1, tiled=True)  8.26 us
    all_to_all x2, starting transfers between devices, monarch_forward(): lax.all_to_all(first, 'blocks', split_axis=1, concat_axis=0, tiled=True)  7.95 us
    dot_general x2, matrix products, monarch_backward(): jnp.einsum('bjt,jkt->jbk', regrouped, grad_out, precision=HIGH)  4.91 us
    unnamed x27, local copies, waits for them, and re-layouts  3.76 us
  transfers between devices with their start and end apart: 4, of which 4 were waited for; matrix products, arithmetic and copies ran while one was open for 12% of the time, Pallas kernels for 0%

commit v1 on v0

--- a/solution.py
+++ b/solution.py
@@ -7,6 +7,12 @@
 COEFF = math.sqrt(2.0 / math.pi)
 EPSILON = 1e-05
 HIGH = lax.Precision.HIGHEST
+
+
+def gather_and_add(value, axis):
+    parts = lax.all_gather(value, axis, axis=0, tiled=False)
+    total = parts.sum(axis=0)
+    return total
 
 
 def gelu_value(values):
@@ -78,7 +84,7 @@
     )
     normalized_gradient = normalized_gradient.reshape(features, tokens)
     gradient_scaled = gain[:, None] * normalized_gradient
-    inner_width = lax.psum(jnp.sum(gradient_scaled * centered_input, axis=0), "blocks")
+    inner_width = gather_and_add(jnp.sum(gradient_scaled * centered_input, axis=0), "blocks")
     input_gradient = cotangent + inverse_root * (
         gradient_scaled - centered_input * (inner_width / feature_width)[None, :]
     )

time: 151 us -> 138 us (0.914)
  blocking collectives: 67.2 us -> 55 us
    psum x1 -> x0, blocking collectives: 32.2 us -> none  [local(): lax.psum(jnp.sum(gradient_scaled * centered_input, axis=0), 'blocks')]
    all_gather x0 -> x1, blocking collectives: none -> 20 us  [gather_and_add(): parts = lax.all_gather(value, axis, axis=0, tiled=False)]
  transfers between devices with their start and end apart: 4 -> 4, of which waited for: 4 -> 4; matrix products, arithmetic and copies ran while one was open for 12% -> 13% of each run, Pallas kernels for 0% -> 0%
where the time goes in v1:
time: 138 us
  blocking collectives  55 us (40%)
  waiting for transfers between devices  39.1 us (28%)
  starting transfers between devices  16.2 us (12%)
  matrix products  15.5 us (11%)
  local copies, waits for them, and re-layouts  8.07 us (6%)
  other arithmetic  2.9 us (2%)
    psum x1, blocking collectives, local(): squares = lax.psum(jnp.sum(activations * activations, axis=0), 'blocks')  35 us
    all_to_all x2, waiting for transfers between devices, monarch_forward(): lax.all_to_all(first, 'blocks', split_axis=1, concat_axis=0, tiled=True)  22.3 us
    all_gather x1, blocking collectives, gather_and_add(): parts = lax.all_gather(value, axis, axis=0, tiled=False)  20 us
    all_to_all x2, waiting for transfers between devices, monarch_backward(): lax.all_to_all(grad_mid, 'blocks', split_axis=0, concat_axis=1, tiled=True)  16.7 us
    all_to_all x2, starting transfers between devices, monarch_backward(): lax.all_to_all(grad_mid, 'blocks', split_axis=0, concat_axis=1, tiled=True)  8.26 us
    all_to_all x2, starting transfers between devices, monarch_forward(): lax.all_to_all(first, 'blocks', split_axis=1, concat_axis=0, tiled=True)  7.95 us
    dot_general x2, matrix products, monarch_backward(): jnp.einsum('bjt,jkt->jbk', regrouped, grad_out, precision=HIGH)  4.91 us
    unnamed x27, local copies, waits for them, and re-layouts  3.76 us
  transfers between devices with their start and end apart: 4, of which 4 were waited for; matrix products, arithmetic and copies ran while one was open for 13% of the time, Pallas kernels for 0%

profile of v1, /device:TPU:0, one launch (start us, length us, event | category | flops | bytes accessed | tf_op | source)
XLA Modules:
  0.0 137.6 jit_solution(9901189688500936383)
XLA Ops:
  0.7 1.2 multiply_reduce_fusion.2
  2.1 35.0 %psum.7 = f32[1024]{0:T(1024)S(1)} all-reduce(f32[1024]{0:T(1024)S(1)} %multiply_reduce_fusion.2), channel_id=1, replica_groups=mesh['groups'=2,'blocks'=16] {'blocks'}, use_global_device_ids=true, to_apply=%region_1.0 | all-reduce | flops 1024 | bytes 8192 | tf_op jit(solution)/shard_map/psum | solution.py:57
  37.1 0.6 copy-done.10
  37.7 0.6 convolution_bitcast_fusion.5
  38.3 1.0 copy.50
  39.4 3.7 %all-to-all-start = ((f32[1,128,1024]{2,0,1:T(1,128)}), f32[1,128,1024]{2,0,1:T(1,128)S(1)}, u32[]{:S(2)}, u32[]{:S(2)}) async-start(f32[1,128,1024]{2,0,1:T(1,128)} %copy.50), calls=%async_computation | async-start | bytes 1048576 | tf_op jit(solution)/shard_map/all_to_all | solution.py:35
  43.1 0.6 convolution_bitcast_fusion.2
  43.7 1.1 copy.56
  44.8 12.5 %all-to-all-done = f32[1,128,1024]{2,0,1:T(1,128)S(1)} async-done(((f32[1,128,1024]{2,0,1:T(1,128)}), f32[1,128,1024]{2,0,1:T(1,128)S(1)}, u32[]{:S(2)}, u32[]{:S(2)}) %all-to-all-start) | async-done | bytes 524320 | tf_op jit(solution)/shard_map/all_to_all | solution.py:35
  57.3 4.1 %all-to-all-start.2 = ((f32[16,8,1024]{2,1,0:T(8,128)}), f32[16,8,1024]{2,1,0:T(8,128)S(1)}, u32[]{:S(2)}, u32[]{:S(2)}) async-start(f32[16,8,1024]{2,1,0:T(8,128)} %copy.56), calls=%async_computation.2 | async-start | bytes 1048576 | tf_op jit(solution)/shard_map/all_to_all | solution.py:43
  61.6 1.8 %add_multiply_fusion = (f32[8,16,1024]{2,1,0:T(8,128)S(1)}, f32[8,16,1024]{2,1,0:T(8,128)}) fusion(f32[8,16,16]{2,1,0:T(8,128)S(1)} %copy-done, f32[16,8,1024]{2,1,0:T(8,128)S(1)} %bitcast.73), kind=kOutput, calls=%fused_computation.37 | convolution fusion | flops 26214400 | bytes 1581056 | tf_op jit(solution)/shard_map/jbk,bjt->jkt/dot_general | solution.py:36
  63.4 1.0 convolution_bitcast_fusion.3
  64.4 1.0 copy.53
  65.4 10.3 %all-to-all-done.2 = f32[16,8,1024]{2,1,0:T(8,128)S(1)} async-done(((f32[16,8,1024]{2,1,0:T(8,128)}), f32[16,8,1024]{2,1,0:T(8,128)S(1)}, u32[]{:S(2)}, u32[]{:S(2)}) %all-to-all-start.2) | async-done | bytes 524320 | tf_op jit(solution)/shard_map/all_to_all | solution.py:43
  75.7 4.2 %all-to-all-start.1 = ((f32[1,128,1024]{2,0,1:T(1,128)}), f32[1,128,1024]{2,0,1:T(1,128)}, u32[]{:S(2)}, u32[]{:S(2)}) async-start(f32[1,128,1024]{2,0,1:T(1,128)} %copy.53), calls=%async_computation.1 | async-start | bytes 1048576 | tf_op jit(solution)/shard_map/all_to_all | solution.py:35
  80.2 0.6 fusion.11
  81.2 0.9 convolution_bitcast_fusion.1
  82.1 1.1 copy.57
  83.2 1.2 fusion
  84.4 9.8 %all-to-all-done.1 = f32[1,128,1024]{2,0,1:T(1,128)} async-done(((f32[1,128,1024]{2,0,1:T(1,128)}), f32[1,128,1024]{2,0,1:T(1,128)}, u32[]{:S(2)}, u32[]{:S(2)}) %all-to-all-start.1) | async-done | bytes 524320 | tf_op jit(solution)/shard_map/all_to_all | solution.py:35
  94.2 4.2 %all-to-all-start.3 = ((f32[16,8,1024]{2,1,0:T(8,128)}), f32[16,8,1024]{2,1,0:T(8,128)S(1)}, u32[]{:S(2)}, u32[]{:S(2)}) async-start(f32[16,8,1024]{2,1,0:T(8,128)} %copy.57), calls=%async_computation.3 | async-start | bytes 1048576 | tf_op jit(solution)/shard_map/all_to_all | solution.py:43
  98.4 3.1 %convolution_multiply_fusion.2 = f32[8,16,16]{2,1,0:T(8,128)} fusion(f32[16,8,1024]{2,1,0:T(8,128)S(1)} %bitcast.74, f32[8,16,1024]{2,1,0:T(8,128)} %bitcast.76, f32[8,16,1024]{2,1,0:T(8,128)} %get-tuple-element.38), kind=kOutput, calls=%fused_computation.9 | convolution fusion | flops 27527168 | bytes 1581056 | tf_op jit(solution)/shard_map/bjt,jkt->jbk/dot_general | solution.py:41
  101.6 1.1 copy.78
  102.7 1.8 %convolution_multiply_fusion = f32[8,16,16]{2,1,0:T(8,128)} fusion(f32[8,16,1024]{2,1,0:T(8,128)S(1)} %bitcast.70, f32[16,8,1024]{2,1,0:T(8,128)S(1)} %bitcast.71), kind=kOutput, calls=%fused_computation.6 | convolution fusion | flops 25167872 | bytes 1056768 | tf_op jit(solution)/shard_map/bjt,jkt->jbk/dot_general | solution.py:41
  104.5 0.9 fusion.14
  105.4 0.9 bitcast_add_fusion
  106.2 6.4 %all-to-all-done.3 = f32[16,8,1024]{2,1,0:T(8,128)S(1)} async-done(((f32[16,8,1024]{2,1,0:T(8,128)}), f32[16,8,1024]{2,1,0:T(8,128)S(1)}, u32[]{:S(2)}, u32[]{:S(2)}) %all-to-all-start.3) | async-done | bytes 524320 | tf_op jit(solution)/shard_map/all_to_all | solution.py:43
  112.7 1.2 multiply_reduce_fusion
  113.9 0.5 broadcast_multiply_fusion.1
  114.4 20.0 %all-gather = f32[16384]{0:T(1024)S(1)} all-gather(f32[1024]{0:T(1024)S(1)} %get-tuple-element.36), channel_id=2, replica_groups=mesh['groups'=2,'blocks'=16] {'blocks'}, dimensions={0}, use_global_device_ids=true | all-gather | bytes 69632 | tf_op jit(solution)/shard_map/all_gather | solution.py:13
  134.8 1.0 copy.61
  135.8 1.8 %fusion.1 = f32[1,128,128]{2,1,0:T(8,128)} fusion(f32[16,8,1024]{2,1,0:T(8,128)S(1)} %all-to-all-done.3, f32[128,1024]{0,1:T(8,128)S(1)} %copy.49, f32[128]{0:T(128)S(1)} %copy-done.10, f32[1024]{0:T(1024)S(1)} %add_rsqrt_fusion), kind=kOutput, calls=%fused_computation.11 | convolution fusion | flops 201605120 | bytes 1118720 | tf_op jit(solution)/shard_map/bit,bjt->bij/dot_general | solution.py:45
  (29 shorter events, 1.4 us)
Async XLA Ops:
  0.6 60.9 %copy-start = (f32[8,16,16]{2,1,0:T(8,128)S(1)}, f32[8,16,16]{2,1,0:T(8,128)}, u32[]{:S(2)}) copy-start(f32[8,16,16]{2,1,0:T(8,128)} %param.11) | copy-start | bytes 24580
  0.6 1.2 copy-start.1
  1.9 35.2 %copy-start.9 = (f32[1,128,128]{2,1,0:T(8,128)S(1)}, f32[1,128,128]{2,1,0:T(8,128)}, u32[]{:S(2)}) copy-start(f32[1,128,128]{2,1,0:T(8,128)} %param.10) | copy-start | bytes 196612
  37.0 0.7 copy-start.10
  39.4 3.7 %copy-start.2 = (f32[128,1024]{1,0:T(8,128)S(1)}, f32[128,1024]{1,0:T(8,128)}, u32[]{:S(2)}) copy-start(f32[128,1024]{1,0:T(8,128)} %param.8) | copy-start | bytes 1572868
  39.4 3.7 %copy-start.8 = (f32[8,16,16]{2,1,0:T(8,128)S(1)}, f32[8,16,16]{2,1,0:T(8,128)}, u32[]{:S(2)}) copy-start(f32[8,16,16]{2,1,0:T(8,128)} %param.13) | copy-start | bytes 24580
  39.4 17.9 %all-to-all-start = ((f32[1,128,1024]{2,0,1:T(1,128)}), f32[1,128,1024]{2,0,1:T(1,128)S(1)}, u32[]{:S(2)}, u32[]{:S(2)}) async-start(f32[1,128,1024]{2,0,1:T(1,128)} %copy.50), calls=%async_computation | async-start | bytes 1048576 | tf_op jit(solution)/shard_map/all_to_all | solution.py:35
  57.3 18.4 %all-to-all-start.2 = ((f32[16,8,1024]{2,1,0:T(8,128)}), f32[16,8,1024]{2,1,0:T(8,128)S(1)}, u32[]{:S(2)}, u32[]{:S(2)}) async-start(f32[16,8,1024]{2,1,0:T(8,128)} %copy.56), calls=%async_computation.2 | async-start | bytes 1048576 | tf_op jit(solution)/shard_map/all_to_all | solution.py:43
  61.5 1.8 %copy-start.3 = (f32[1,128,1024]{2,1,0:T(8,128)}, f32[1,128,1024]{2,1,0:T(8,128)S(1)}, u32[]{:S(2)}) copy-start(f32[1,128,1024]{2,1,0:T(8,128)S(1)} %copy.79) | copy-start | bytes 1572868
  61.5 1.8 %copy-start.7 = (f32[1,128,128]{2,1,0:T(8,128)S(1)}, f32[1,128,128]{2,1,0:T(8,128)}, u32[]{:S(2)}) copy-start(f32[1,128,128]{2,1,0:T(8,128)} %param.12) | copy-start | bytes 196612
  75.7 18.5 %all-to-all-start.1 = ((f32[1,128,1024]{2,0,1:T(1,128)}), f32[1,128,1024]{2,0,1:T(1,128)}, u32[]{:S(2)}, u32[]{:S(2)}) async-start(f32[1,128,1024]{2,0,1:T(1,128)} %copy.53), calls=%async_computation.1 | async-start | bytes 1048576 | tf_op jit(solution)/shard_map/all_to_all | solution.py:35
  80.1 1.0 copy-start.5
  80.8 1.3 copy-start.6
  84.4 14.0 %copy-start.4 = (f32[1,128,1024]{2,1,0:T(8,128)S(1)}, f32[1,128,1024]{2,1,0:T(8,128)}, u32[]{:S(2)}) copy-start(f32[1,128,1024]{2,1,0:T(8,128)} %copy-done.3) | copy-start | bytes 1572868
  94.2 18.4 %all-to-all-start.3 = ((f32[16,8,1024]{2,1,0:T(8,128)}), f32[16,8,1024]{2,1,0:T(8,128)S(1)}, u32[]{:S(2)}, u32[]{:S(2)}) async-start(f32[16,8,1024]{2,1,0:T(8,128)} %copy.57), calls=%async_computation.3 | async-start | bytes 1048576 | tf_op jit(solution)/shard_map/all_to_all | solution.py:43
